TPU v7x, 32 devices: a whole 2x2x4 slice. The times are simulated.
32 devices in a mesh: layer: 8 (over z, core), space: 4 (over y, x).
Axes of the slice: x: 2, y: 2, z: 4, core: 2. Of those that a mesh axis runs over, the one named last changes fastest.
Arguments:
- initial: float32 [32, 4, 1024], P(None, 'space'), may hold values from -6 to 6
- kernels: bfloat16 [16, 27, 32, 32], P('layer'), may hold values from -0.21875 to 0.21875
- biases: float32 [16, 32], P('layer'), may hold values from -3 to 3
Outputs:
- states: float32 [16, 32, 4, 1024], P('layer', None, 'space')
All inputs are finite; a program needn't handle non-finite values.
Results may differ from a plain program's by a relative error of at most 0.0041.
Values may be sent and summed in bfloat16 or wider, within the bound.
A program may use at most 64 MiB of HBM per device.

v0:
```python
import functools

import jax
import jax.numpy as jnp
from jax import lax
from jax.experimental import pallas as pl
from jax.experimental.pallas import tpu as pltpu
from jax.sharding import PartitionSpec as P

NZ = 64
CYCLES = 2
STEP = 0.125
MESH = pl.DeviceIdType.MESH

W1, W2, W4, U0, U1 = range(5)
DISTANCE = (1, 2, 4, 1, 2)
SOURCE = (2, 2, 2, 0, 1)


def kernel(
    layers,
    slabs,
    init_ref,
    ker_ref,
    bias_ref,
    out_ref,
    weights,
    bias_col,
    init_hi,
    init_f,
    point_hi,
    point_f,
    run,
    t_init,
    t_near,
    t_last,
    msg_hi,
    msg_lo,
    out_hi,
    out_lo,
    gather_send,
    gather_recv,
    send_hi,
    send_lo,
    recv_hi,
    recv_lo,
):
    chans, cells = init_ref.shape
    body_rows = slabs * chans
    rank = lax.axis_index("layer")
    slab = lax.axis_index("space")
    is_even = rank % 2 == 0
    is_first = rank % 4 == 1
    is_coarse = rank % 4 == 3
    depth = jnp.where(is_even, 0, jnp.where(is_first, 1, 2))
    reach = jnp.where(is_even, 1, jnp.where(is_first, 2, 4))

    barrier = pltpu.get_barrier_semaphore()
    for off in range(1, slabs):
        pl.semaphore_signal(
            barrier,
            inc=1,
            device_id=(rank, (slab + off) % slabs),
            device_id_type=MESH,
        )
    pairs = ((1, True, True), (2, rank % 2 == 1, rank % 2 == 1), (4, is_coarse, is_coarse))
    expected = slabs - 1
    for dist, ok_up, ok_down in pairs:
        up = jnp.logical_and(ok_up, rank + dist < layers)
        down = jnp.logical_and(ok_down, rank - dist >= 0)

        @pl.when(up)
        def _():
            pl.semaphore_signal(
                barrier, inc=1, device_id=(rank + dist, slab), device_id_type=MESH
            )

        @pl.when(down)
        def _():
            pl.semaphore_signal(
                barrier, inc=1, device_id=(rank - dist, slab), device_id_type=MESH
            )

        expected = expected + jnp.where(up, 1, 0) + jnp.where(down, 1, 0)

    own_rows = pl.ds(pl.multiple_of((slab + 1) * chans, chans), chans)
    init_hi[own_rows, :] = init_ref[...].astype(jnp.bfloat16)
    pl.semaphore_wait(barrier, expected)

    def gather_copy(off):
        return pltpu.make_async_remote_copy(
            src_ref=init_hi.at[own_rows, :],
            dst_ref=init_hi.at[own_rows, :],
            send_sem=gather_send.at[off],
            recv_sem=gather_recv.at[off],
            device_id=(rank, (slab + off) % slabs),
            device_id_type=MESH,
        )

    for off in range(1, slabs):
        gather_copy(off).start()

    for which in range(2):
        for be in range(9):
            weights[which, be * chans : (be + 1) * chans, :] = jnp.concatenate(
                [ker_ref[which, a * 9 + be] for a in range(3)], axis=1
            )
        rows = lax.broadcasted_iota(jnp.int32, (chans, chans), 0)
        cols = lax.broadcasted_iota(jnp.int32, (chans, chans), 1)
        spread = jnp.where(rows == cols, bias_ref[which : which + 1, :], 0.0)
        bias_col[which] = jnp.broadcast_to(jnp.sum(spread, axis=1, keepdims=True), (chans, 128))
    empty = jnp.zeros((chans, cells), jnp.bfloat16)
    for buf in (init_hi, point_hi):
        buf[0:chans, :] = empty
        buf[body_rows + chans : body_rows + 2 * chans, :] = empty
    for cyc in range(CYCLES):
        for kind in range(5):
            msg_hi[cyc, kind, 0:chans, :] = empty
            msg_hi[cyc, kind, body_rows + chans : body_rows + 2 * chans, :] = empty

    column = lax.broadcasted_iota(jnp.int32, (chans, cells), 1)
    in_z = column % NZ

    def bent(view, which, p):
        window = view[pl.ds(pl.multiple_of(p * chans, chans), 3 * chans), :]
        parts = jnp.dot(weights[which], window, preferred_element_type=jnp.float32)
        total = None
        for e in range(3):
            q = [parts[(3 * b + e) * chans : (3 * b + e + 1) * chans] for b in range(3)]
            lined = (
                q[1]
                + jnp.where(column >= NZ, pltpu.roll(q[0], NZ, 1), 0.0)
                + jnp.where(column < cells - NZ, pltpu.roll(q[2], cells - NZ, 1), 0.0)
            )
            if e == 0:
                lined = jnp.where(in_z > 0, pltpu.roll(lined, 1, 1), 0.0)
            if e == 2:
                lined = jnp.where(in_z < NZ - 1, pltpu.roll(lined, cells - 1, 1), 0.0)
            total = lined if total is None else total + lined
        return jnp.tanh(total + bias_col[which][:, 0:1])

    def plane(view, p):
        return view[pl.ds(pl.multiple_of((p + 1) * chans, chans), chans), :]

    def held(cyc, kind, p):
        low = jnp.where(p == slab, msg_lo[cyc, kind].astype(jnp.float32), 0.0)
        return plane(msg_hi.at[cyc, kind], p).astype(jnp.float32) + low

    def copies(cyc, kind):
        target = (rank + DISTANCE[kind], slab)
        src = SOURCE[kind]
        high = pltpu.make_async_remote_copy(
            src_ref=out_hi.at[cyc, src],
            dst_ref=msg_hi.at[cyc, kind, pl.ds(chans, body_rows), :],
            send_sem=send_hi.at[cyc, kind],
            recv_sem=recv_hi.at[cyc, kind],
            device_id=target,
            device_id_type=MESH,
        )
        low = pltpu.make_async_remote_copy(
            src_ref=out_lo.at[cyc, src],
            dst_ref=msg_lo.at[cyc, kind],
            send_sem=send_lo.at[cyc, kind],
            recv_sem=recv_lo.at[cyc, kind],
            device_id=target,
            device_id_type=MESH,
        )
        return high, low

    def sends(cyc, kind):
        final = cyc == CYCLES - 1
        fits = rank + DISTANCE[kind] < layers
        if kind == W1:
            return fits
        if kind == W2:
            return jnp.logical_and(fits, is_coarse if final else rank % 2 == 1)
        if kind == W4:
            return jnp.logical_and(fits, is_coarse)
        if kind == U0:
            return jnp.logical_and(fits, is_even)
        return jnp.logical_and(fits, is_first)

    def send(cyc, kind):
        @pl.when(sends(cyc, kind))
        def _():
            for copy in copies(cyc, kind):
                copy.start()

    def arrive(cyc, kind):
        for copy in copies(cyc, kind):
            copy.wait_recv()

    def publish(cyc, src, p, value):
        high = value.astype(jnp.bfloat16)
        out_hi[cyc, src, pl.ds(pl.multiple_of(p * chans, chans), chans), :] = high

        @pl.when(p == slab)
        def _():
            out_lo[cyc, src] = (value - high.astype(jnp.float32)).astype(jnp.bfloat16)

    def each_plane(step):
        def body(p, carry):
            step(p)
            return carry

        lax.fori_loop(0, slabs, body, 0)

    def publish_all(cyc, src):
        each_plane(lambda p: publish(cyc, src, p, run[p]))

    for off in range(1, slabs):
        gather_copy(off).wait_recv()

    def spread_init(p):
        init_f[p] = plane(init_hi, p).astype(jnp.float32)

        @pl.when(p == slab)
        def _():
            init_f[p] = init_ref[...]

    each_plane(spread_init)

    for cyc in range(CYCLES):
        if cyc == 0:

            def odd_step(p):
                value = init_f[p] + STEP * bent(init_hi, 0, p)
                point_f[p] = value
                point_hi[pl.ds(pl.multiple_of((p + 1) * chans, chans), chans), :] = value.astype(
                    jnp.bfloat16
                )

            each_plane(odd_step)
        else:

            @pl.when(jnp.logical_and(rank > 0, depth > 0))
            def _():
                arrive(cyc - 1, W1)

            @pl.when(rank > 0)
            def _():
                near = msg_hi.at[cyc - 1, W1]

                def odd_step(p):
                    value = held(cyc - 1, W1, p) + STEP * bent(near, 0, p)
                    point_f[p] = value
                    point_hi[
                        pl.ds(pl.multiple_of((p + 1) * chans, chans), chans), :
                    ] = value.astype(jnp.bfloat16)

                each_plane(odd_step)

        def even_step(p):
            value = point_f[p] + STEP * bent(point_hi, 1, p)
            run[p] = value
            publish(cyc, 0, p, value)

        each_plane(even_step)
        send(cyc, U0)
        if cyc == 0:

            def base_step(p):
                t_init[p] = bent(init_hi, 1, p)

            each_plane(base_step)
        else:

            @pl.when(depth > 0)
            def _():
                def near_step(p):
                    t_near[p] = bent(msg_hi.at[cyc - 1, W1], 1, p)

                each_plane(near_step)

        @pl.when(rank % 2 == 1)
        def _():
            arrive(cyc, U0)

            def step(p):
                fresh = bent(msg_hi.at[cyc, U0], 1, p)
                if cyc == 0:
                    old, t_old = init_f[p], t_init[p]
                else:
                    old, t_old = held(cyc - 1, W1, p), t_near[p]
                value = run[p] + (held(cyc, U0, p) - old) + 2 * STEP * (fresh - t_old)
                run[p] = value
                publish(cyc, 1, p, value)

            each_plane(step)

        send(cyc, U1)

        @pl.when(is_coarse)
        def _():
            if cyc > 0:
                arrive(cyc - 1, W2)

                def near_step(p):
                    t_near[p] = bent(msg_hi.at[cyc - 1, W2], 1, p)

                each_plane(near_step)
            arrive(cyc, U1)

            def step(p):
                fresh = bent(msg_hi.at[cyc, U1], 1, p)
                if cyc == 0:
                    old, t_old = init_f[p], t_init[p]
                else:
                    old, t_old = held(cyc - 1, W2, p), t_near[p]
                run[p] = run[p] + (held(cyc, U1, p) - old) + 4 * STEP * (fresh - t_old)

            each_plane(step)

        @pl.when(rank >= reach)
        def _():
            for kind in (W1, W2, W4):

                @pl.when(depth == kind)
                def _():
                    arrive(cyc, kind)

            size = jnp.where(is_even, 2 * STEP, jnp.where(is_first, 4 * STEP, 8 * STEP))

            def step(p):
                fresh = bent(msg_hi.at[cyc, depth], 1, p)
                if cyc == 0:
                    old, t_old = init_f[p], t_init[p]
                else:
                    old, t_old = held(cyc - 1, depth, p), t_last[p]
                value = run[p] + (held(cyc, depth, p) - old) + size * (fresh - t_old)
                run[p] = value
                if cyc < CYCLES - 1:
                    t_last[p] = fresh

            each_plane(step)

        publish_all(cyc, 2)
        send(cyc, W2)
        send(cyc, W1)
        send(cyc, W4)

    last = CYCLES - 1
    out_ref[1] = run[slab]

    @pl.when(rank == 0)
    def _():
        out_ref[0] = point_f[slab]

    @pl.when(rank > 0)
    def _():
        @pl.when(depth > 0)
        def _():
            arrive(last, W1)

        out_ref[0] = held(last, W1, slab) + STEP * bent(msg_hi.at[last, W1], 0, slab)

    for off in range(1, slabs):
        gather_copy(off).wait_send()
    for cyc in range(CYCLES):
        for kind in range(5):

            @pl.when(sends(cyc, kind))
            def _():
                for copy in copies(cyc, kind):
                    copy.wait_send()


def on_device(initial, kernels, biases):
    layers = lax.axis_size("layer")
    slabs = lax.axis_size("space")
    chans, _, cells = initial.shape
    rows = (slabs + 2) * chans
    f32, b16 = jnp.float32, jnp.bfloat16
    field = pltpu.VMEM((slabs, chans, cells), f32)
    out = pl.pallas_call(
        functools.partial(kernel, layers, slabs),
        out_shape=jax.ShapeDtypeStruct((2, chans, cells), f32),
        in_specs=[pl.BlockSpec(memory_space=pltpu.VMEM)] * 3,
        out_specs=pl.BlockSpec(memory_space=pltpu.VMEM),
        scratch_shapes=[
            pltpu.VMEM((2, 9 * chans, 3 * chans), b16),
            pltpu.VMEM((2, chans, 128), f32),
            pltpu.VMEM((rows, cells), b16),
            field,
            pltpu.VMEM((rows, cells), b16),
            field,
            field,
            field,
            field,
            field,
            pltpu.VMEM((CYCLES, 5, rows, cells), b16),
            pltpu.VMEM((CYCLES, 5, chans, cells), b16),
            pltpu.VMEM((CYCLES, 3, slabs * chans, cells), b16),
            pltpu.VMEM((CYCLES, 3, chans, cells), b16),
            pltpu.SemaphoreType.DMA((slabs,)),
            pltpu.SemaphoreType.DMA((slabs,)),
            pltpu.SemaphoreType.DMA((CYCLES, 5)),
            pltpu.SemaphoreType.DMA((CYCLES, 5)),
            pltpu.SemaphoreType.DMA((CYCLES, 5)),
            pltpu.SemaphoreType.DMA((CYCLES, 5)),
        ],
        compiler_params=pltpu.CompilerParams(
            collective_id=0, has_side_effects=True, vmem_limit_bytes=60 * 1024 * 1024
        ),
    )(initial.reshape(chans, cells), kernels, biases)
    return out.reshape(2, chans, 1, cells)


def solution(mesh):
    return jax.shard_map(
        on_device,
        mesh=mesh,
        in_specs=(P(None, "space", None), P("layer", None, None, None), P("layer", None)),
        out_specs=P("layer", None, "space", None),
        check_vma=False,
    )
```

profile of v0, /device:TPU:25, one launch (start us, length us, event | category | flops | bytes accessed | tf_op | source)
XLA Modules:
  0.0 69.0 jit_solution(10897566810706683682)
XLA Ops:
  0.0 1.6 %copy.7 = f32[32,1,1024]{2,0,1:T(8,128)} copy(f32[32,1,1024]{2,1,0:T(1,128)} %param.3) | data formatting | bytes 262144
  1.6 65.5 %shard_map.37 = f32[2,32,1024]{2,1,0:T(8,128)} custom-call(f32[32,1024]{1,0:T(8,128)} %bitcast.5, bf16[2,27,32,32]{3,2,1,0:T(8,128)(2,1)} %ker_ref.1, f32[2,32]{1,0:T(2,128)} %bias_ref.1), custom_call_target="tpu_custom_call" | custom-call | tf_op jit(solution)/shard_map/pallas_call | solution.py:375
  67.1 1.9 %copy.4 = f32[2,32,1,1024]{3,2,1,0:T(1,128)} copy(f32[2,32,1,1024]{3,1,0,2:T(8,128)} %bitcast.4) | data formatting | bytes 524288 | tf_op jit(solution)/shard_map/reshape | solution.py:406
where the time goes:
time: 69.2 us; the launch traced here: 69 us
  Pallas kernels  65.5 us (95%)
  local copies, waits for them, and re-layouts  3.51 us (5%)
    pallas_call x1, Pallas kernels, on_device(): pl.pallas_call(functools.partial(kernel, layers, slabs), out_shape=jax.Sh...  65.5 us
    reshape x1, local copies, waits for them, and re-layouts, on_device(): return out.reshape(2, chans, 1, cells)  1.92 us
    unnamed x1, local copies, waits for them, and re-layouts  1.58 us

commit v1 on v0

v1 whole, which is shorter than its diff:
```python
import functools

import jax
import jax.numpy as jnp
from jax import lax
from jax.experimental import pallas as pl
from jax.experimental.pallas import tpu as pltpu
from jax.sharding import PartitionSpec as P

NZ = 64
CYCLES = 2
STEP = 0.125
MESH = pl.DeviceIdType.MESH

W1, W2, W4, U0, U1 = range(5)
DISTANCE = (1, 2, 4, 1, 2)
SOURCE = (2, 2, 2, 0, 1)


def kernel(
    layers,
    slabs,
    init_ref,
    ker_ref,
    bias_ref,
    out_ref,
    weights,
    bias_col,
    init_hi,
    init_f,
    point_f,
    run,
    t_init,
    t_near,
    t_two,
    t_last,
    wide_point,
    wide_msg,
    wide_near,
    msg_hi,
    msg_lo,
    out_hi,
    out_lo,
    gather_send,
    gather_recv,
    send_hi,
    send_lo,
    recv_hi,
    recv_lo,
):
    chans, _, cells = init_ref.shape
    body_rows = slabs * chans
    rank = lax.axis_index("layer")
    slab = lax.axis_index("space")
    is_even = rank % 2 == 0
    is_first = rank % 4 == 1
    is_coarse = rank % 4 == 3
    depth = jnp.where(is_even, 0, jnp.where(is_first, 1, 2))
    reach = jnp.where(is_even, 1, jnp.where(is_first, 2, 4))

    barrier = pltpu.get_barrier_semaphore()
    for off in range(1, slabs):
        pl.semaphore_signal(
            barrier,
            inc=1,
            device_id=(rank, (slab + off) % slabs),
            device_id_type=MESH,
        )
    pairs = ((1, True, True), (2, rank % 2 == 1, rank % 2 == 1), (4, is_coarse, is_coarse))
    expected = slabs - 1
    for dist, ok_up, ok_down in pairs:
        up = jnp.logical_and(ok_up, rank + dist < layers)
        down = jnp.logical_and(ok_down, rank - dist >= 0)

        @pl.when(up)
        def _():
            pl.semaphore_signal(
                barrier, inc=1, device_id=(rank + dist, slab), device_id_type=MESH
            )

        @pl.when(down)
        def _():
            pl.semaphore_signal(
                barrier, inc=1, device_id=(rank - dist, slab), device_id_type=MESH
            )

        expected = expected + jnp.where(up, 1, 0) + jnp.where(down, 1, 0)

    own_rows = pl.ds(pl.multiple_of((slab + 1) * chans, chans), chans)
    own_init = init_ref[:, 0, :]
    init_hi[own_rows, :] = own_init.astype(jnp.bfloat16)
    pl.semaphore_wait(barrier, expected)

    def gather_copy(off):
        return pltpu.make_async_remote_copy(
            src_ref=init_hi.at[own_rows, :],
            dst_ref=init_hi.at[own_rows, :],
            send_sem=gather_send.at[off],
            recv_sem=gather_recv.at[off],
            device_id=(rank, (slab + off) % slabs),
            device_id_type=MESH,
        )

    for off in range(1, slabs):
        gather_copy(off).start()

    for which in range(2):
        for b in range(3):
            weights[which, b * chans : (b + 1) * chans, :] = jnp.concatenate(
                [ker_ref[which, 9 * a + 3 * b + e] for a in range(3) for e in range(3)], axis=1
            )
        rows = lax.broadcasted_iota(jnp.int32, (chans, chans), 0)
        cols = lax.broadcasted_iota(jnp.int32, (chans, chans), 1)
        spread = jnp.where(rows == cols, bias_ref[which : which + 1, :], 0.0)
        bias_col[which] = jnp.broadcast_to(jnp.sum(spread, axis=1, keepdims=True), (chans, 128))
    empty = jnp.zeros((3 * chans, cells), jnp.bfloat16)
    wide_rows = 3 * chans
    for buf in (wide_point, wide_msg, wide_near):
        buf[0:wide_rows, :] = empty
        buf[(slabs + 1) * wide_rows : (slabs + 2) * wide_rows, :] = empty

    in_z = lax.broadcasted_iota(jnp.int32, (chans, cells), 1) % NZ
    half = lax.broadcasted_iota(jnp.int32, (chans, 2 * NZ), 1) >= NZ
    tiles = cells // (2 * NZ)

    def widen(wide, p, field):
        field = field.astype(jnp.float32)
        before = jnp.where(in_z > 0, pltpu.roll(field, 1, 1), 0.0)
        after = jnp.where(in_z < NZ - 1, pltpu.roll(field, cells - 1, 1), 0.0)
        for e, part in enumerate((before, field, after)):
            start = pl.multiple_of((p + 1) * wide_rows + e * chans, chans)
            wide[pl.ds(start, chans), :] = part.astype(jnp.bfloat16)

    def bent(wide, which, p):
        window = wide[pl.ds(pl.multiple_of(p * wide_rows, wide_rows), 3 * wide_rows), :]
        parts = jnp.dot(weights[which], window, preferred_element_type=jnp.float32)

        def tile(b, j):
            return parts[b * chans : (b + 1) * chans, j * 2 * NZ : (j + 1) * 2 * NZ]

        cols = []
        for j in range(tiles):
            upper = tile(2, j) + tile(0, j - 1) if j > 0 else tile(2, j)
            lower = tile(0, j) + tile(2, j + 1) if j < tiles - 1 else tile(0, j)
            sides = pltpu.roll(jnp.where(half, upper, lower), NZ, 1)
            cols.append(tile(1, j) + sides)
        return jnp.tanh(jnp.concatenate(cols, axis=1) + bias_col[which][:, 0:1])

    def plane(view, p):
        return view[pl.ds(pl.multiple_of((p + 1) * chans, chans), chans), :]

    def held(cyc, kind, p):
        low = msg_lo[cyc, kind, p].astype(jnp.float32)
        return plane(msg_hi.at[cyc, kind], p).astype(jnp.float32) + low

    def copies(cyc, kind, p, source=0, distance=1):
        target = (rank + distance, slab)
        high = pltpu.make_async_remote_copy(
            src_ref=out_hi.at[cyc, source, pl.ds(pl.multiple_of(p * chans, chans), chans), :],
            dst_ref=msg_hi.at[cyc, kind, pl.ds(pl.multiple_of((p + 1) * chans, chans), chans), :],
            send_sem=send_hi.at[cyc, kind, p],
            recv_sem=recv_hi.at[cyc, kind, p],
            device_id=target,
            device_id_type=MESH,
        )
        low = pltpu.make_async_remote_copy(
            src_ref=out_lo.at[cyc, source],
            dst_ref=msg_lo.at[cyc, kind, slab],
            send_sem=send_lo.at[cyc, kind],
            recv_sem=recv_lo.at[cyc, kind],
            device_id=target,
            device_id_type=MESH,
        )
        return high, low

    def sends(cyc, kind):
        final = cyc == CYCLES - 1
        fits = rank + DISTANCE[kind] < layers
        if kind == W1:
            return fits
        if kind == W2:
            return jnp.logical_and(fits, is_coarse if final else rank % 2 == 1)
        if kind == W4:
            return jnp.logical_and(fits, is_coarse)
        if kind == U0:
            return jnp.logical_and(fits, is_even)
        return jnp.logical_and(fits, is_first)

    def send_plane(cyc, kind, p):
        @pl.when(sends(cyc, kind))
        def _():
            high, low = copies(cyc, kind, p, SOURCE[kind], DISTANCE[kind])
            high.start()

            @pl.when(p == slab)
            def _():
                low.start()

    def arrive(cyc, kind, p):
        high, low = copies(cyc, kind, p)
        high.wait_recv()

        @pl.when(p == slab)
        def _():
            low.wait_recv()

    def publish(cyc, src, p, value):
        high = value.astype(jnp.bfloat16)
        out_hi[cyc, src, pl.ds(pl.multiple_of(p * chans, chans), chans), :] = high

        @pl.when(p == slab)
        def _():
            out_lo[cyc, src] = (value - high.astype(jnp.float32)).astype(jnp.bfloat16)

        if src == 0:
            send_plane(cyc, U0, p)
        if src == 1:
            send_plane(cyc, U1, p)
        if src == 2:
            @pl.when(is_coarse)
            def _():
                send_plane(cyc, W2, p)

            @pl.when(jnp.logical_not(is_coarse))
            def _():
                send_plane(cyc, W1, p)

    def each_plane(step):
        def body(p, carry):
            step(p)
            return carry

        lax.fori_loop(0, slabs, body, 0)

    def staged(load, step):
        def body(p, carry):
            @pl.when(p < slabs)
            def _():
                load(p)

            @pl.when(p > 0)
            def _():
                step(p - 1)

            return carry

        lax.fori_loop(0, slabs + 1, body, 0)

    def receive(cyc, kind, wide):
        def load(p):
            arrive(cyc, kind, p)
            widen(wide, p, plane(msg_hi.at[cyc, kind], p))

        return load

    def clear_low(p):
        @pl.when(p != slab)
        def _():
            for cyc in range(CYCLES):
                for kind in range(5):
                    msg_lo[cyc, kind, p] = empty[:chans]

    each_plane(clear_low)
    for off in range(1, slabs):
        gather_copy(off).wait_recv()

    def load_init(p):
        high = plane(init_hi, p)
        widen(wide_near, p, high)
        init_f[p] = high.astype(jnp.float32)

        @pl.when(p == slab)
        def _():
            init_f[p] = own_init

    def set_point(p, value):
        point_f[p] = value
        widen(wide_point, p, value.astype(jnp.bfloat16))

    last = CYCLES - 1
    for cyc in range(CYCLES):
        if cyc == 0:
            staged(load_init, lambda p: set_point(p, init_f[p] + STEP * bent(wide_near, 0, p)))
        else:

            @pl.when(is_coarse)
            def _():
                def two_step(p):
                    t_two[p] = bent(wide_msg, 1, p)

                staged(receive(cyc - 1, W2, wide_msg), two_step)

            @pl.when(rank > 0)
            def _():
                def load(p):
                    @pl.when(depth > 0)
                    def _():
                        arrive(cyc - 1, W1, p)

                    widen(wide_near, p, plane(msg_hi.at[cyc - 1, W1], p))

                staged(
                    load,
                    lambda p: set_point(
                        p, held(cyc - 1, W1, p) + STEP * bent(wide_near, 0, p)
                    ),
                )

        def even_step(p):
            value = point_f[p] + STEP * bent(wide_point, 1, p)
            run[p] = value
            publish(cyc, 0, p, value)

        each_plane(even_step)
        if cyc == 0:

            def base_step(p):
                t_init[p] = bent(wide_near, 1, p)

            each_plane(base_step)
        else:

            @pl.when(depth > 0)
            def _():
                def near_step(p):
                    t_near[p] = bent(wide_near, 1, p)

                each_plane(near_step)

        @pl.when(rank % 2 == 1)
        def _():
            def step(p):
                fresh = bent(wide_msg, 1, p)
                if cyc == 0:
                    old, t_old = init_f[p], t_init[p]
                else:
                    old, t_old = held(cyc - 1, W1, p), t_near[p]
                value = run[p] + (held(cyc, U0, p) - old) + 2 * STEP * (fresh - t_old)
                run[p] = value
                publish(cyc, 1, p, value)

            staged(receive(cyc, U0, wide_msg), step)

        @pl.when(is_coarse)
        def _():
            def step(p):
                fresh = bent(wide_msg, 1, p)
                if cyc == 0:
                    old, t_old = init_f[p], t_init[p]
                else:
                    old, t_old = held(cyc - 1, W2, p), t_two[p]
                run[p] = run[p] + (held(cyc, U1, p) - old) + 4 * STEP * (fresh - t_old)

            staged(receive(cyc, U1, wide_msg), step)

        @pl.when(rank >= reach)
        def _():
            size = jnp.where(is_even, 2 * STEP, jnp.where(is_first, 4 * STEP, 8 * STEP))

            def step(p):
                fresh = bent(wide_msg, 1, p)
                if cyc == 0:
                    old, t_old = init_f[p], t_init[p]
                else:
                    old, t_old = held(cyc - 1, depth, p), t_last[p]
                value = run[p] + (held(cyc, depth, p) - old) + size * (fresh - t_old)
                run[p] = value
                publish(cyc, 2, p, value)
                if cyc < last:
                    t_last[p] = fresh

            staged(receive(cyc, depth, wide_msg), step)

        @pl.when(rank < reach)
        def _():
            each_plane(lambda p: publish(cyc, 2, p, run[p]))

        @pl.when(is_coarse)
        def _():
            each_plane(lambda p: send_plane(cyc, W1, p))
            each_plane(lambda p: send_plane(cyc, W4, p))

        if cyc < last:

            @pl.when(is_first)
            def _():
                each_plane(lambda p: send_plane(cyc, W2, p))

    out_ref[1, :, 0, :] = run[slab]

    @pl.when(rank == 0)
    def _():
        out_ref[0, :, 0, :] = point_f[slab]

    @pl.when(rank > 0)
    def _():
        def load(p):
            @pl.when(depth > 0)
            def _():
                arrive(last, W1, p)

            widen(wide_msg, p, plane(msg_hi.at[last, W1], p))

        each_plane(load)
        out_ref[0, :, 0, :] = held(last, W1, slab) + STEP * bent(wide_msg, 0, slab)

    for off in range(1, slabs):
        gather_copy(off).wait_send()
    for cyc in range(CYCLES):
        for kind in range(5):

            @pl.when(sends(cyc, kind))
            def _():
                def done(p):
                    high, low = copies(cyc, kind, p, SOURCE[kind], DISTANCE[kind])
                    high.wait_send()

                    @pl.when(p == slab)
                    def _():
                        low.wait_send()

                each_plane(done)


def on_device(initial, kernels, biases):
    layers = lax.axis_size("layer")
    slabs = lax.axis_size("space")
    chans, _, cells = initial.shape
    rows = (slabs + 2) * chans
    f32, b16 = jnp.float32, jnp.bfloat16
    field = pltpu.VMEM((slabs, chans, cells), f32)
    return pl.pallas_call(
        functools.partial(kernel, layers, slabs),
        out_shape=jax.ShapeDtypeStruct((2, chans, 1, cells), f32),
        in_specs=[pl.BlockSpec(memory_space=pltpu.VMEM)] * 3,
        out_specs=pl.BlockSpec(memory_space=pltpu.VMEM),
        scratch_shapes=[
            pltpu.VMEM((2, 3 * chans, 9 * chans), b16),
            pltpu.VMEM((2, chans, 128), f32),
            pltpu.VMEM((rows, cells), b16),
            field,
            field,
            field,
            field,
            field,
            field,
            field,
            pltpu.VMEM((3 * rows, cells), b16),
            pltpu.VMEM((3 * rows, cells), b16),
            pltpu.VMEM((3 * rows, cells), b16),
            pltpu.VMEM((CYCLES, 5, rows, cells), b16),
            pltpu.VMEM((CYCLES, 5, slabs, chans, cells), b16),
            pltpu.VMEM((CYCLES, 3, slabs * chans, cells), b16),
            pltpu.VMEM((CYCLES, 3, chans, cells), b16),
            pltpu.SemaphoreType.DMA((slabs,)),
            pltpu.SemaphoreType.DMA((slabs,)),
            pltpu.SemaphoreType.DMA((CYCLES, 5, slabs)),
            pltpu.SemaphoreType.DMA((CYCLES, 5)),
            pltpu.SemaphoreType.DMA((CYCLES, 5, slabs)),
            pltpu.SemaphoreType.DMA((CYCLES, 5)),
        ],
        compiler_params=pltpu.CompilerParams(
            collective_id=0, has_side_effects=True, vmem_limit_bytes=60 * 1024 * 1024
        ),
    )(initial, kernels, biases)


def solution(mesh):
    return jax.shard_map(
        on_device,
        mesh=mesh,
        in_specs=(P(None, "space", None), P("layer", None, None, None), P("layer", None)),
        out_specs=P("layer", None, "space", None),
        check_vma=False,
    )
```

time: 69.2 us -> 54.5 us (0.79)
  Pallas kernels: 65.5 us -> 52.6 us
  local copies, waits for them, and re-layouts: 3.51 us -> 1.67 us
    pallas_call x1, Pallas kernels: 65.5 us -> 52.6 us  [on_device(): pl.pallas_call(functools.partial(kernel, layers, slabs), out_shape=jax.Sh...]
    reshape x1 -> x0, local copies, waits for them, and re-layouts: 1.92 us -> none  [on_device(): return out.reshape(2, chans, 1, cells)]
where the time goes in v1:
time: 54.5 us; the launch traced here: 54.3 us
  Pallas kernels  52.6 us (97%)
  local copies, waits for them, and re-layouts  1.67 us (3%)
    pallas_call x1, Pallas kernels, on_device(): pl.pallas_call(functools.partial(kernel, layers, slabs), out_shape=jax.Sh...  52.6 us
    unnamed x1, local copies, waits for them, and re-layouts  1.67 us

profile of v1, /device:TPU:25, one launch (start us, length us, event | category | flops | bytes accessed | tf_op | source)
XLA Modules:
  0.0 54.3 jit_solution(956953488702365075)
XLA Ops:
  0.0 52.6 %shard_map.37 = f32[2,32,1,1024]{3,2,1,0:T(1,128)} custom-call(f32[32,1,1024]{2,1,0:T(1,128)} %init_ref.1, bf16[2,27,32,32]{3,2,1,0:T(8,128)(2,1)} %ker_ref.1, f32[2,32]{1,0:T(2,128)} %bias_ref.1), custom_call_target="tpu_custom_call" | custom-call | tf_op jit(solution)/shard_map/pallas_call | solution.py:432
  52.6 1.7 %copy.5 = f32[2,32,1,1024]{3,2,1,0:T(1,128)} copy(f32[2,32,1,1024]{3,2,1,0:T(1,128)} %shard_map.37) | data formatting | bytes 524288

commit v2 on v1

--- a/solution.py
+++ b/solution.py
@@ -10,11 +10,18 @@
 NZ = 64
 CYCLES = 2
 STEP = 0.125
+GROUP = 2
+UNROLL = 4
 MESH = pl.DeviceIdType.MESH
 
 W1, W2, W4, U0, U1 = range(5)
 DISTANCE = (1, 2, 4, 1, 2)
 SOURCE = (2, 2, 2, 0, 1)
+
+
+def rows_at(index, size, count=1):
+    start = index * size
+    return pl.ds(start if isinstance(start, int) else pl.multiple_of(start, size), count * size)
 
 
 def kernel(
@@ -128,11 +135,10 @@
         before = jnp.where(in_z > 0, pltpu.roll(field, 1, 1), 0.0)
         after = jnp.where(in_z < NZ - 1, pltpu.roll(field, cells - 1, 1), 0.0)
         for e, part in enumerate((before, field, after)):
-            start = pl.multiple_of((p + 1) * wide_rows + e * chans, chans)
-            wide[pl.ds(start, chans), :] = part.astype(jnp.bfloat16)
+            wide[rows_at(3 * (p + 1) + e, chans), :] = part.astype(jnp.bfloat16)
 
     def bent(wide, which, p):
-        window = wide[pl.ds(pl.multiple_of(p * wide_rows, wide_rows), 3 * wide_rows), :]
+        window = wide[rows_at(p, wide_rows, 3), :]
         parts = jnp.dot(weights[which], window, preferred_element_type=jnp.float32)
 
         def tile(b, j):
@@ -147,7 +153,7 @@
         return jnp.tanh(jnp.concatenate(cols, axis=1) + bias_col[which][:, 0:1])
 
     def plane(view, p):
-        return view[pl.ds(pl.multiple_of((p + 1) * chans, chans), chans), :]
+        return view[rows_at(p + 1, chans), :]
 
     def held(cyc, kind, p):
         low = msg_lo[cyc, kind, p].astype(jnp.float32)
@@ -156,8 +162,8 @@
     def copies(cyc, kind, p, source=0, distance=1):
         target = (rank + distance, slab)
         high = pltpu.make_async_remote_copy(
-            src_ref=out_hi.at[cyc, source, pl.ds(pl.multiple_of(p * chans, chans), chans), :],
-            dst_ref=msg_hi.at[cyc, kind, pl.ds(pl.multiple_of((p + 1) * chans, chans), chans), :],
+            src_ref=out_hi.at[cyc, source, rows_at(p, chans), :],
+            dst_ref=msg_hi.at[cyc, kind, rows_at(p + 1, chans), :],
             send_sem=send_hi.at[cyc, kind, p],
             recv_sem=recv_hi.at[cyc, kind, p],
             device_id=target,
@@ -204,19 +210,22 @@
         def _():
             low.wait_recv()
 
-    def publish(cyc, src, p, value):
-        high = value.astype(jnp.bfloat16)
-        out_hi[cyc, src, pl.ds(pl.multiple_of(p * chans, chans), chans), :] = high
-
+    def store(cyc, src, p, value):
+        run[p] = value
+        out_hi[cyc, src, rows_at(p, chans), :] = value.astype(jnp.bfloat16)
+
+    def publish(cyc, src, p):
         @pl.when(p == slab)
         def _():
-            out_lo[cyc, src] = (value - high.astype(jnp.float32)).astype(jnp.bfloat16)
+            high = out_hi[cyc, src, rows_at(p, chans), :].astype(jnp.float32)
+            out_lo[cyc, src] = (run[p] - high).astype(jnp.bfloat16)
 
         if src == 0:
             send_plane(cyc, U0, p)
         if src == 1:
             send_plane(cyc, U1, p)
         if src == 2:
+
             @pl.when(is_coarse)
             def _():
                 send_plane(cyc, W2, p)
@@ -225,33 +234,53 @@
             def _():
                 send_plane(cyc, W1, p)
 
-    def each_plane(step):
+    def loop(first, end, step):
         def body(p, carry):
             step(p)
             return carry
 
-        lax.fori_loop(0, slabs, body, 0)
-
-    def staged(load, step):
-        def body(p, carry):
-            @pl.when(p < slabs)
-            def _():
-                load(p)
-
-            @pl.when(p > 0)
-            def _():
-                step(p - 1)
-
-            return carry
-
-        lax.fori_loop(0, slabs + 1, body, 0)
-
-    def receive(cyc, kind, wide):
-        def load(p):
-            arrive(cyc, kind, p)
-            widen(wide, p, plane(msg_hi.at[cyc, kind], p))
-
-        return load
+        lax.fori_loop(first, end, body, 0)
+
+    def each_plane(step):
+        loop(0, slabs, step)
+
+    def grouped(step, after=None, wait=None, prepare=None, group=GROUP):
+        if slabs > UNROLL:
+            if wait is not None:
+                each_plane(wait)
+            if prepare is not None:
+                each_plane(prepare)
+            each_plane(step)
+            if after is not None:
+                each_plane(after)
+            return
+        done = prepared = 0
+        for p in range(slabs):
+            if wait is not None:
+                wait(p)
+            ready = p if p < slabs - 1 else slabs
+            if ready - done >= group or p == slabs - 1:
+                if prepare is not None:
+                    for q in range(prepared, p + 1):
+                        prepare(q)
+                for q in range(done, ready):
+                    step(q)
+                if after is not None:
+                    for q in range(done, ready):
+                        after(q)
+                done, prepared = ready, p + 1
+
+    def received(cyc, kind, wide, step, after=None, guard=None):
+        def wait(p):
+            if guard is None:
+                arrive(cyc, kind, p)
+            else:
+
+                @pl.when(guard)
+                def _():
+                    arrive(cyc, kind, p)
+
+        grouped(step, after, wait, lambda p: widen(wide, p, plane(msg_hi.at[cyc, kind], p)))
 
     def clear_low(p):
         @pl.when(p != slab)
@@ -264,14 +293,14 @@
     for off in range(1, slabs):
         gather_copy(off).wait_recv()
 
-    def load_init(p):
-        high = plane(init_hi, p)
-        widen(wide_near, p, high)
-        init_f[p] = high.astype(jnp.float32)
-
-        @pl.when(p == slab)
-        def _():
-            init_f[p] = own_init
+    init_f[slab] = own_init
+
+    def copy_init(p):
+        @pl.when(p != slab)
+        def _():
+            init_f[p] = plane(init_hi, p).astype(jnp.float32)
+
+    each_plane(copy_init)
 
     def set_point(p, value):
         point_f[p] = value
@@ -280,7 +309,11 @@
     last = CYCLES - 1
     for cyc in range(CYCLES):
         if cyc == 0:
-            staged(load_init, lambda p: set_point(p, init_f[p] + STEP * bent(wide_near, 0, p)))
+            grouped(
+                lambda p: set_point(p, init_f[p] + STEP * bent(wide_near, 0, p)),
+                prepare=lambda p: widen(wide_near, p, plane(init_hi, p)),
+                group=slabs,
+            )
         else:
 
             @pl.when(is_coarse)
@@ -288,36 +321,30 @@
                 def two_step(p):
                     t_two[p] = bent(wide_msg, 1, p)
 
-                staged(receive(cyc - 1, W2, wide_msg), two_step)
+                received(cyc - 1, W2, wide_msg, two_step)
 
             @pl.when(rank > 0)
             def _():
-                def load(p):
-                    @pl.when(depth > 0)
-                    def _():
-                        arrive(cyc - 1, W1, p)
-
-                    widen(wide_near, p, plane(msg_hi.at[cyc - 1, W1], p))
-
-                staged(
-                    load,
+                received(
+                    cyc - 1,
+                    W1,
+                    wide_near,
                     lambda p: set_point(
                         p, held(cyc - 1, W1, p) + STEP * bent(wide_near, 0, p)
                     ),
+                    guard=depth > 0,
                 )
 
         def even_step(p):
-            value = point_f[p] + STEP * bent(wide_point, 1, p)
-            run[p] = value
-            publish(cyc, 0, p, value)
-
-        each_plane(even_step)
+            store(cyc, 0, p, point_f[p] + STEP * bent(wide_point, 1, p))
+
+        grouped(even_step, lambda p: publish(cyc, 0, p))
         if cyc == 0:
 
             def base_step(p):
                 t_init[p] = bent(wide_near, 1, p)
 
-            each_plane(base_step)
+            grouped(base_step, group=slabs)
         else:
 
             @pl.when(depth > 0)
@@ -325,7 +352,7 @@
                 def near_step(p):
                     t_near[p] = bent(wide_near, 1, p)
 
-                each_plane(near_step)
+                grouped(near_step, group=slabs)
 
         @pl.when(rank % 2 == 1)
         def _():
@@ -336,10 +363,9 @@
                 else:
                     old, t_old = held(cyc - 1, W1, p), t_near[p]
                 value = run[p] + (held(cyc, U0, p) - old) + 2 * STEP * (fresh - t_old)
-                run[p] = value
-                publish(cyc, 1, p, value)
-
-            staged(receive(cyc, U0, wide_msg), step)
+                store(cyc, 1, p, value)
+
+            received(cyc, U0, wide_msg, step, lambda p: publish(cyc, 1, p))
 
         @pl.when(is_coarse)
         def _():
@@ -351,7 +377,7 @@
                     old, t_old = held(cyc - 1, W2, p), t_two[p]
                 run[p] = run[p] + (held(cyc, U1, p) - old) + 4 * STEP * (fresh - t_old)
 
-            staged(receive(cyc, U1, wide_msg), step)
+            received(cyc, U1, wide_msg, step)
 
         @pl.when(rank >= reach)
         def _():
@@ -364,16 +390,19 @@
                 else:
                     old, t_old = held(cyc - 1, depth, p), t_last[p]
                 value = run[p] + (held(cyc, depth, p) - old) + size * (fresh - t_old)
-                run[p] = value
-                publish(cyc, 2, p, value)
+                store(cyc, 2, p, value)
                 if cyc < last:
                     t_last[p] = fresh
 
-            staged(receive(cyc, depth, wide_msg), step)
+            received(cyc, depth, wide_msg, step, lambda p: publish(cyc, 2, p))
 
         @pl.when(rank < reach)
         def _():
-            each_plane(lambda p: publish(cyc, 2, p, run[p]))
+            def keep(p):
+                store(cyc, 2, p, run[p])
+                publish(cyc, 2, p)
+
+            each_plane(keep)
 
         @pl.when(is_coarse)
         def _():

time: 54.5 us -> 50.5 us (0.927)
  Pallas kernels: 52.6 us -> 48.7 us
    pallas_call x1, Pallas kernels: 52.6 us -> 48.7 us  [on_device(): pl.pallas_call(functools.partial(kernel, layers, slabs), out_shape=jax.Sh...]
where the time goes in v2:
time: 50.5 us; the launch traced here: 50.4 us
  Pallas kernels  48.7 us (96%)
  local copies, waits for them, and re-layouts  1.67 us (3%)
    pallas_call x1, Pallas kernels, on_device(): pl.pallas_call(functools.partial(kernel, layers, slabs), out_shape=jax.Sh...  48.7 us
    unnamed x1, local copies, waits for them, and re-layouts  1.67 us

profile of v2, /device:TPU:25, one launch (start us, length us, event | category | flops | bytes accessed | tf_op | source)
XLA Modules:
  0.0 50.4 jit_solution(15248880658956493105)
XLA Ops:
  0.0 48.7 %shard_map.37 = f32[2,32,1,1024]{3,2,1,0:T(1,128)} custom-call(f32[32,1,1024]{2,1,0:T(1,128)} %init_ref.1, bf16[2,27,32,32]{3,2,1,0:T(8,128)(2,1)} %ker_ref.1, f32[2,32]{1,0:T(2,128)} %bias_ref.1), custom_call_target="tpu_custom_call" | custom-call | tf_op jit(solution)/shard_map/pallas_call | solution.py:461
  48.7 1.7 %copy.5 = f32[2,32,1,1024]{3,2,1,0:T(1,128)} copy(f32[2,32,1,1024]{3,2,1,0:T(1,128)} %shard_map.37) | data formatting | bytes 524288
